TPU v7x, 128 devices: a whole 4x4x4 slice. The times are simulated.
128 devices in a mesh: dp: 8 (over y, core), prompt: 16 (over x, z).
Axes of the slice: x: 4, y: 4, z: 4, core: 2. Of those that a mesh axis runs over, the one named last changes fastest.
Arguments:
- cand_hidden: bfloat16 [16, 8, 128, 1024], P('prompt', 'dp')
- ref_hidden: bfloat16 [32, 16, 128, 1024], P('dp', 'prompt')
- cand_ids: int32 [16, 8, 128], P('prompt', 'dp'), may hold values from 0 to 50264
- ref_ids: int32 [32, 16, 128], P('dp', 'prompt'), may hold values from 0 to 50264
- cand_len: int32 [16, 8], P('prompt', 'dp'), may hold values from 32 to 128
- reference_length: int32 [32, 16], P('dp', 'prompt'), may hold values from 32 to 128
- idf_table: float32 [50265], replicated, may hold values from 1 to 10
- up_weight: bfloat16 [1024, 4096], replicated, may hold values from -0.1875 to 0.1875
- up_bias: float32 [4096], replicated, may hold values from -3 to 3
- down_weight: bfloat16 [4096, 1024], replicated, may hold values from -0.09375 to 0.09375
- down_bias: float32 [1024], replicated, may hold values from -3 to 3
- norm_gain: float32 [1024], replicated, may hold values from 0.3 to 3
- norm_bias: float32 [1024], replicated, may hold values from -3 to 3
- pair_cand: int32 [8, 16, 32], P('dp', 'prompt'), may hold values from 0 to 7
- pair_ref: int32 [8, 16, 32], P('dp', 'prompt'), may hold values from 0 to 63
- pair_count: int32 [8, 16], P('dp', 'prompt'), may hold values from 8 to 32, as said below
Outputs:
- pair_scores: float32 [3, 8, 16, 32], P(None, 'dp', 'prompt')
- totals: float32 [3], replicated
Inputs may be any that keep to these rules, and one draw needn't show every extreme that they name: Slots from pair_count on are not live; some device has all 32 slots live.
All inputs are finite; a program needn't handle non-finite values.
Results may differ from a plain program's by a relative error of at most 0.0003.
Values may be sent and summed in bfloat16 or wider, within the bound.
No kernel may reach another device: no remote copies, remote signals or barrier semaphores. Data moves between devices by JAX's collectives and lax.ppermute only.
A program may use at most 128 MiB of HBM per device.

v0:
```python
import jax
import jax.numpy as jnp
from jax import lax
from jax.sharding import PartitionSpec as P


def encode_rows(hidden, up_weight, up_bias, down_weight, down_bias, norm_gain, norm_bias):
    preactivation_hidden = jnp.dot(hidden, up_weight, preferred_element_type=jnp.float32) + up_bias
    activated = jax.nn.gelu(preactivation_hidden, approximate=False).astype(jnp.bfloat16)
    summed = (
        hidden.astype(jnp.float32)
        + jnp.dot(activated, down_weight, preferred_element_type=jnp.float32)
        + down_bias
    )
    center = jnp.mean(summed, axis=-1, keepdims=True)
    spread = jnp.mean(jnp.square(summed - center), axis=-1, keepdims=True)
    normed = (summed - center) * lax.rsqrt(spread + 1e-05) * norm_gain + norm_bias
    magnitude = jnp.sum(jnp.square(normed), axis=-1, keepdims=True)
    return (normed * lax.rsqrt(magnitude + 1e-06)).astype(jnp.bfloat16)


def token_idf_weights(ids, lengths, idf_table):
    positions = jnp.arange(ids.shape[-1], dtype=jnp.int32)
    live_tokens = positions[None, :] < lengths[:, None]
    return jnp.where(live_tokens, jnp.take(idf_table, ids, axis=0), 0.0).astype(jnp.bfloat16)


def on_device(
    cand_hidden,
    ref_hidden,
    cand_ids,
    ref_ids,
    cand_len,
    reference_length,
    idf_table,
    up_weight,
    up_bias,
    down_weight,
    down_bias,
    norm_gain,
    norm_bias,
    pair_cand,
    pair_ref,
    pair_count,
):
    seq_len = cand_hidden.shape[2]
    width = cand_hidden.shape[3]

    def encode_side(hidden, ids, lengths):
        units = encode_rows(
            hidden.reshape(-1, width),
            up_weight,
            up_bias,
            down_weight,
            down_bias,
            norm_gain,
            norm_bias,
        )
        weights = token_idf_weights(ids.reshape(-1, seq_len), lengths.reshape(-1), idf_table)
        return (units.reshape(hidden.shape), weights.reshape(hidden.shape[:3]))

    ref_unit, ref_weight = encode_side(ref_hidden, ref_ids, reference_length)
    candidate_normalized, cand_weight = encode_side(cand_hidden, cand_ids, cand_len)
    cand_all, cand_wall = (
        lax.all_gather(candidate_normalized, "dp", axis=1, tiled=True),
        lax.all_gather(cand_weight, "dp", axis=1, tiled=True),
    )
    cand_all = cand_all.reshape(-1, seq_len, width)
    cand_wall = cand_wall.reshape(-1, seq_len)
    cand_pick = pair_cand.reshape(-1)
    slot_total = cand_pick.shape[0]
    ref_pick = pair_ref.reshape(-1)
    groups = lax.axis_size("prompt")
    ref_major = ref_pick // groups
    ref_minor = ref_pick % groups
    order = jnp.argsort(ref_minor, stable=True)
    sorted_minor = jnp.take(ref_minor, order, axis=0)
    sorted_major = jnp.take(ref_major, order, axis=0)
    sorted_cand = jnp.take(cand_pick, order, axis=0)
    paired_normalized = jnp.take(cand_all, sorted_cand, axis=0)
    pair_weight = jnp.take(cand_wall, sorted_cand, axis=0)
    initial = (
        jnp.zeros((slot_total, seq_len), jnp.float32),
        jnp.zeros((slot_total, seq_len), jnp.float32),
        jnp.zeros((slot_total, seq_len), jnp.bfloat16),
    )
    ref_all, ref_wall = (
        lax.all_gather(ref_unit, "prompt", axis=1, tiled=True),
        lax.all_gather(ref_weight, "prompt", axis=1, tiled=True),
    )
    shard_span = ref_all.shape[1]
    inside = (sorted_minor >= 0) & (sorted_minor < 0 + shard_span)
    within = sorted_major * shard_span + jnp.clip(sorted_minor - 0, 0, shard_span - 1)
    selected_normalized = jnp.take(ref_all.reshape(-1, seq_len, width), within, axis=0)
    chosen_weight = jnp.take(ref_wall.reshape(-1, seq_len), within, axis=0)
    cosine_similarity = jnp.einsum(
        "uqg,uog->uqo", paired_normalized, selected_normalized, preferred_element_type=jnp.float32
    )
    row_best = jnp.max(
        jnp.where(chosen_weight[:, None, :] > 0, cosine_similarity, -10000.0), axis=2
    )
    col_best = jnp.max(jnp.where(pair_weight[:, :, None] > 0, cosine_similarity, -10000.0), axis=1)
    keeper = inside[:, None]
    updated = []
    for stored, fresh in zip(initial, (row_best, col_best, chosen_weight)):
        updated.append(jnp.where(keeper, fresh, stored))
    row_best, col_best, ref_chosen = tuple(updated)
    cand_float = pair_weight.astype(jnp.float32)
    ref_float = ref_chosen.astype(jnp.float32)
    precision_sorted = jnp.sum(cand_float * row_best, axis=1) / jnp.sum(cand_float, axis=1)
    recall_sorted = jnp.sum(ref_float * col_best, axis=1) / jnp.sum(ref_float, axis=1)
    inverse = jnp.argsort(order)
    precision = jnp.take(precision_sorted, inverse, axis=0)
    recall = jnp.take(recall_sorted, inverse, axis=0)
    fmeasure = 2.0 * precision * recall / jnp.maximum(precision + recall, 0.7)
    live_slots = jnp.arange(slot_total, dtype=jnp.int32) < pair_count.reshape(1)
    stacked = jnp.where(live_slots[None, :], jnp.stack([precision, recall, fmeasure]), 0.0)
    score_sums, live_total = lax.psum(
        (jnp.sum(stacked, axis=1), jnp.sum(live_slots.astype(jnp.float32))), ("dp", "prompt")
    )
    return (stacked.reshape(3, 1, 1, slot_total), score_sums / live_total)


def solution(mesh):
    placed = (
        P("prompt", "dp", None, None),
        P("dp", "prompt", None, None),
        P("prompt", "dp", None),
        P("dp", "prompt", None),
        P("prompt", "dp"),
        P("dp", "prompt"),
        P(),
        P(),
        P(),
        P(),
        P(),
        P(),
        P(),
        P("dp", "prompt", None),
        P("dp", "prompt", None),
        P("dp", "prompt"),
    )
    return jax.shard_map(
        on_device,
        mesh=mesh,
        in_specs=placed,
        out_specs=(P(None, "dp", "prompt", None), P()),
        check_vma=False,
    )
```

profile of v0, /device:TPU:1, one launch (start us, length us, event | category | flops | bytes accessed | tf_op | source)
XLA Modules:
  0.0 263.4 jit_solution(12290140118969234346)
XLA Ops:
  7.2 0.0 copy-start
  7.2 0.0 copy-start.2
  7.2 0.0 copy-start.3
  7.2 0.0 all-gather.6.cloned.1.call-start
  7.2 13.2 %fusion.169 = (f32[128]{0:T(128)S(1)}, f32[128,1024]{1,0:T(8,128)S(1)}) fusion(f32[1024]{0:T(1024)} %param.30, bf16[4096,1024]{1,0:T(8,128)(2,1)} %param.29, bf16[1024,4096]{1,0:T(8,128)(2,1)} %param.27, f32[4096]{0:T(1024)} %param.28, bf16[1,1,128,1024]{3,2,1,0:T(8,128)(2,1)} %param.20), kind=kOutput, calls=%fused_computation.264 | convolution fusion | flops 2182610944 | bytes 17584640 | tf_op jit(solution)/shard_map/dot_general | solution.py:12
  20.5 0.0 copy-start.7
  20.5 0.0 copy-start.8
  20.5 0.0 copy-start.9
  20.5 0.2 multiply_reduce_fusion.3
  20.7 0.0 copy-done.2
  20.7 0.0 copy-done.3
  20.7 0.3 multiply_reduce_fusion.2
  21.0 0.9 multiply_convert_fusion.1
  21.9 0.0 all-gather.6.cloned.1.call-update
  21.9 0.2 all-gather.4.cloned.1.call-start
  22.1 0.0 copy-done.7
  22.2 0.0 copy-done.8
  22.2 0.0 copy-done.9
  22.2 30.3 %fusion.168 = (f32[512]{0:T(512)S(1)}, f32[512,1024]{1,0:T(8,128)S(1)}) fusion(f32[1024]{0:T(1024)S(1)} %copy-done.9, bf16[4096,1024]{1,0:T(8,128)(2,1)} %param.29, bf16[512,1024]{1,0:T(8,128)(2,1)S(1)} %bitcast.84, bf16[1024,4096]{1,0:T(8,128)(2,1)} %param.27, f32[4096]{0:T(1024)S(1)} %copy-done.8), kind=kOutput, calls=%fused_computation.263 | convolution fusion | flops 8730443776 | bytes 19945472 | tf_op jit(solution)/shard_map/dot_general | solution.py:12
  52.5 0.4 multiply_reduce_fusion.1
  52.8 0.9 multiply_reduce_fusion
  53.7 0.0 copy-start.6
  53.7 0.0 copy-start.10
  53.8 1.5 multiply_convert_fusion
  55.2 0.0 copy-start.1
  55.2 0.0 copy-start.4
  55.2 0.0 copy-start.5
  55.2 0.0 all-gather.4.cloned.1.call-update
  56.6 0.0 copy-done.6
  56.6 0.0 copy-done
  56.6 1.1 gather_fusion
  57.8 12.1 %all_gather.12 = bf16[1,8,128]{2,0,1:T(2,128)(2,1)S(1)} all-gather(bf16[1,1,128]{2,0,1:T(2,128)(2,1)S(1)} %fusion.100), channel_id=1, replica_groups=mesh['dp'=8,'prompt'=16] {'dp'}, dimensions={1}, use_global_device_ids=true | all-gather | bytes 2304 | tf_op jit(solution)/shard_map/all_gather | solution.py:66
  69.8 0.0 copy-done.10
  69.9 1.6 sort.34
  71.5 0.7 gather_fusion.7
  72.2 0.7 gather_fusion.8
  72.9 0.0 copy-done.1
  72.9 0.7 gather_fusion.6
  73.6 0.0 copy-done.4
  73.6 3.1 %gather_fusion.2 = bf16[512]{0:T(512)(128)(2,1)S(1)} fusion(f32[50265]{0:T(1024)S(1)} %copy-done, s32[1024]{0:T(1024)S(1)} %pad_clamp_fusion.2), kind=kCustom, calls=%fused_computation.7 | custom fusion | bytes 4096 | tf_op jit(solution)/shard_map/jit(_take)/gather | solution.py:25
  76.8 0.0 copy-done.5
  76.8 0.1 fusion.98
  76.8 20.3 %all_gather.13 = bf16[4,16,128]{2,0,1:T(4,128)(2,1)S(1)} all-gather(bf16[4,1,128]{2,0,1:T(4,128)(2,1)S(1)} %fusion.98), channel_id=1, replica_groups=mesh['dp'=8,'prompt'=16] {'prompt'}, dimensions={1}, use_global_device_ids=true | all-gather | bytes 17408 | tf_op jit(solution)/shard_map/all_gather | solution.py:89
  97.2 1.6 sort.35
  98.8 0.6 convert_reduce_fusion.2
  99.4 0.6 gather_fusion.1
  100.0 0.6 gather_fusion.3
  100.6 0.1 broadcast_compare_fusion
  100.7 0.1 broadcast_compare_fusion.1
  100.8 0.0 all-gather.6.cloned.1.call-done
  100.8 6.9 %gather_fusion.4 = bf16[32,128,1024]{2,1,0:T(8,128)(2,1)} fusion(bf16[8,128,1024]{2,1,0:T(8,128)(2,1)} %bitcast.74, s32[1024]{0:T(1024)S(1)} %get-tuple-element.39), kind=kCustom, calls=%fused_computation.9 | custom fusion | bytes 16777344 | tf_op jit(solution)/shard_map/jit(_take)/gather | solution.py:80
  107.7 62.4 %all-gather.4.cloned.1.call-done = bf16[4,16,128,1024]{3,2,1,0:T(8,128)(2,1)} async-done(((bf16[4,1,128,1024]{3,2,1,0:T(8,128)(2,1)}), bf16[4,16,128,1024]{3,2,1,0:T(8,128)(2,1)}) %all-gather.4.cloned.1.call-update) | async-done | bytes 16777232 | tf_op jit(solution)/shard_map/all_gather | solution.py:88
  170.1 10.8 %gather_fusion.5 = bf16[32,128,1024]{2,1,0:T(8,128)(2,1)} fusion(bf16[64,128,1024]{2,1,0:T(8,128)(2,1)} %bitcast.75, s32[1024]{0:T(1024)S(1)} %get-tuple-element.38), kind=kCustom, calls=%fused_computation.10 | custom fusion | bytes 16777344 | tf_op jit(solution)/shard_map/jit(_take)/gather | solution.py:94
  180.8 7.5 %select_reduce_fusion = (f32[32,128]{1,0:T(8,128)S(1)}, f32[32,128]{1,0:T(8,128)S(1)}) fusion(pred[32,128]{1,0:T(8,128)(4,1)S(1)} %broadcast_compare_fusion, pred[32,128]{1,0:T(8,128)(4,1)S(1)} %broadcast_compare_fusion.1, bf16[32,128,1024]{2,1,0:T(8,128)(2,1)} %gather_fusion.5, pred[32]{0:T(512)(128)(4,1)S(1)} %get-tuple-element.22, ...), kind=kOutput, calls=%fused_computation.73 | convolution fusion | flops 1084219392 | bytes 16818240 | tf_op jit(solution)/shard_map/uqg,uog->uqo/dot_general | solution.py:96
  188.4 0.2 convert_reduce_fusion.1
  188.6 0.7 gather_fusion.9
  189.3 0.7 gather_fusion.10
  190.1 0.1 fusion.96
  190.2 64.7 %all-reduce = (f32[3]{0:T(128)S(1)}, f32[]{:T(128)}) all-reduce(f32[3]{0:T(128)S(1)} %fusion.96, f32[]{:T(128)} %convert_reduce_fusion.2), channel_id=1, replica_groups=mesh['dp'=8,'prompt'=16] {'dp','prompt'}, use_global_device_ids=true, to_apply=%region_15.18 | all-reduce | flops 4 | bytes 32 | tf_op jit(solution)/shard_map/psum | solution.py:118
  254.9 1.2 broadcast_divide_fusion
  256.0 0.6 broadcast_select_fusion.3
  (28 shorter events, 0.2 us)
Async XLA Ops:
  7.2 49.4 %copy-start = (f32[50265]{0:T(1024)S(1)}, f32[50265]{0:T(1024)}, u32[]{:S(2)}) copy-start(f32[50265]{0:T(1024)} %param.26) | copy-start | bytes 603184
  7.2 13.5 %copy-start.2 = (f32[1024]{0:T(1024)S(1)}, f32[1024]{0:T(1024)}, u32[]{:S(2)}) copy-start(f32[1024]{0:T(1024)} %param.32) | copy-start | bytes 12292
  7.2 13.5 %copy-start.3 = (f32[1024]{0:T(1024)S(1)}, f32[1024]{0:T(1024)}, u32[]{:S(2)}) copy-start(f32[1024]{0:T(1024)} %param.31) | copy-start | bytes 12292
  7.2 93.6 %all-gather.6.cloned.1.call-start = ((), (), s32[]{:S(2)}) async-start(), calls=%async_computation.1 | async-start | bytes 2359296 | tf_op jit(solution)/shard_map/all_gather | solution.py:65
  20.5 1.7 copy-start.7
  20.5 1.7 copy-start.8
  20.5 1.7 copy-start.9
  21.9 148.1 %all-gather.4.cloned.1.call-start = ((), (), s32[]{:S(2)}) async-start(), calls=%async_computation | async-start | bytes 17825792 | tf_op jit(solution)/shard_map/all_gather | solution.py:88
  53.7 2.8 %copy-start.6 = (s32[1,1,128]{2,1,0:T(1,128)S(1)}, s32[1,1,128]{2,1,0:T(1,128)}, u32[]{:S(2)}) copy-start(s32[1,1,128]{2,1,0:T(1,128)} %param.22) | copy-start | bytes 1540
  53.7 16.1 %copy-start.10 = (s32[1,1,32]{2,1,0:T(1,128)S(1)}, s32[1,1,32]{2,1,0:T(1,128)}, u32[]{:S(2)}) copy-start(s32[1,1,32]{2,1,0:T(1,128)} %param.34) | copy-start | bytes 388
  55.2 17.7 %copy-start.1 = (s32[1,1,32]{2,1,0:T(1,128)S(1)}, s32[1,1,32]{2,1,0:T(1,128)}, u32[]{:S(2)}) copy-start(s32[1,1,32]{2,1,0:T(1,128)} %param.33) | copy-start | bytes 388
  55.2 18.4 %copy-start.4 = (s32[4,1,128]{2,1,0:T(1,128)S(1)}, s32[4,1,128]{2,1,0:T(1,128)}, u32[]{:S(2)}) copy-start(s32[4,1,128]{2,1,0:T(1,128)} %param.23) | copy-start | bytes 6148
  55.2 21.6 %copy-start.5 = (s32[4,1]{0,1:T(1,128)S(1)}, s32[4,1]{0,1:T(1,128)}, u32[]{:S(2)}) copy-start(s32[4,1]{0,1:T(1,128)} %param.25) | copy-start | bytes 52
Sparse Core Ops, SparseCore 0:
  22.0 28.8 all-gather.5
  55.4 114.6 all-gather.3
where the time goes:
time: 264 us; the launch traced here: 263 us
  blocking collectives  97 us (37%)
  waiting for transfers between devices  62.4 us (24%)
  matrix products  51 us (19%)
  local copies, waits for them, and re-layouts  26.7 us (10%)
  between operations  15.6 us (6%)
  other arithmetic  10.3 us (4%)
    psum x1, blocking collectives, on_device(): lax.psum((jnp.sum(stacked, axis=1), jnp.sum(live_slots.astype(jnp.float32...  64.7 us
    all_gather x1, waiting for transfers between devices, on_device(): lax.all_gather(ref_unit, 'prompt', axis=1, tiled=True)  62.4 us
    dot_general x2, matrix products, encode_rows(): jnp.dot(activated, down_weight, preferred_element_type=jnp.float32)  43.5 us
    all_gather x1, blocking collectives, on_device(): lax.all_gather(ref_weight, 'prompt', axis=1, tiled=True)  20.3 us
    all_gather x1, blocking collectives, on_device(): lax.all_gather(cand_weight, 'dp', axis=1, tiled=True)  12.1 us
    gather x1, local copies, waits for them, and re-layouts, on_device(): jnp.take(ref_all.reshape(-1, seq_len, width), within, axis=0)  10.8 us
    dot_general x1, matrix products, on_device(): jnp.einsum('uqg,uog->uqo', paired_normalized, selected_normalized, prefer...  7.55 us
    gather x1, local copies, waits for them, and re-layouts, on_device(): paired_normalized = jnp.take(cand_all, sorted_cand, axis=0)  6.87 us
  transfers between devices with their start and end apart: 2, of which 1 were waited for; matrix products, arithmetic and copies ran while one was open for 20% of the time, Pallas kernels for 0%

commit v1 on v0

--- a/solution.py
+++ b/solution.py
@@ -115,8 +115,13 @@
     fmeasure = 2.0 * precision * recall / jnp.maximum(precision + recall, 0.7)
     live_slots = jnp.arange(slot_total, dtype=jnp.int32) < pair_count.reshape(1)
     stacked = jnp.where(live_slots[None, :], jnp.stack([precision, recall, fmeasure]), 0.0)
-    score_sums, live_total = lax.psum(
-        (jnp.sum(stacked, axis=1), jnp.sum(live_slots.astype(jnp.float32))), ("dp", "prompt")
+
+    def track_core_over_axis(base_x):
+        local_now = lax.psum(lax.psum(base_x, axis_name="prompt"), "dp")
+        return local_now
+
+    score_sums, live_total = track_core_over_axis(
+        (jnp.sum(stacked, axis=1), jnp.sum(live_slots.astype(jnp.float32)))
     )
     return (stacked.reshape(3, 1, 1, slot_total), score_sums / live_total)
 

time: 264 us -> 251 us (0.951)
  blocking collectives: 97 us -> 84.5 us
    psum x1 -> x2, blocking collectives: 64.7 us -> 52.2 us  [track_core_over_axis(): local_now = lax.psum(lax.psum(base_x, axis_name='prompt'), 'dp')]
  transfers between devices with their start and end apart: 2 -> 2, of which waited for: 1 -> 1; matrix products, arithmetic and copies ran while one was open for 20% -> 21% of each run, Pallas kernels for 0% -> 0%
where the time goes in v1:
time: 251 us
  blocking collectives  84.5 us (34%)
  waiting for transfers between devices  62.4 us (25%)
  matrix products  51 us (20%)
  local copies, waits for them, and re-layouts  26.7 us (11%)
  between operations  15.6 us (6%)
  other arithmetic  10.3 us (4%)
    all_gather x1, waiting for transfers between devices, on_device(): lax.all_gather(ref_unit, 'prompt', axis=1, tiled=True)  62.4 us
    psum x2, blocking collectives, track_core_over_axis(): local_now = lax.psum(lax.psum(base_x, axis_name='prompt'), 'dp')  52.2 us
    dot_general x2, matrix products, encode_rows(): jnp.dot(activated, down_weight, preferred_element_type=jnp.float32)  43.5 us
    all_gather x1, blocking collectives, on_device(): lax.all_gather(ref_weight, 'prompt', axis=1, tiled=True)  20.3 us
    all_gather x1, blocking collectives, on_device(): lax.all_gather(cand_weight, 'dp', axis=1, tiled=True)  12.1 us
    gather x1, local copies, waits for them, and re-layouts, on_device(): jnp.take(ref_all.reshape(-1, seq_len, width), within, axis=0)  10.8 us
    dot_general x1, matrix products, on_device(): jnp.einsum('uqg,uog->uqo', paired_normalized, selected_normalized, prefer...  7.55 us
    gather x1, local copies, waits for them, and re-layouts, on_device(): paired_normalized = jnp.take(cand_all, sorted_cand, axis=0)  6.87 us
  transfers between devices with their start and end apart: 2, of which 1 were waited for; matrix products, arithmetic and copies ran while one was open for 21% of the time, Pallas kernels for 0%

profile of v1, /device:TPU:1, one launch (start us, length us, event | category | flops | bytes accessed | tf_op | source)
XLA Modules:
  0.0 250.9 jit_solution(16127311340115645470)
XLA Ops:
  7.2 0.0 copy-start
  7.2 0.0 copy-start.2
  7.2 0.0 copy-start.3
  7.2 0.0 all-gather.6.cloned.1.call-start
  7.2 13.2 %fusion.169 = (f32[128]{0:T(128)S(1)}, f32[128,1024]{1,0:T(8,128)S(1)}) fusion(f32[1024]{0:T(1024)} %param.30, bf16[4096,1024]{1,0:T(8,128)(2,1)} %param.29, bf16[1024,4096]{1,0:T(8,128)(2,1)} %param.27, f32[4096]{0:T(1024)} %param.28, bf16[1,1,128,1024]{3,2,1,0:T(8,128)(2,1)} %param.20), kind=kOutput, calls=%fused_computation.264 | convolution fusion | flops 2182610944 | bytes 17584640 | tf_op jit(solution)/shard_map/dot_general | solution.py:12
  20.5 0.0 copy-start.7
  20.5 0.0 copy-start.8
  20.5 0.0 copy-start.9
  20.5 0.2 multiply_reduce_fusion.3
  20.7 0.0 copy-done.2
  20.7 0.0 copy-done.3
  20.7 0.3 multiply_reduce_fusion.2
  21.0 0.9 multiply_convert_fusion.1
  21.9 0.0 all-gather.6.cloned.1.call-update
  21.9 0.2 all-gather.4.cloned.1.call-start
  22.1 0.0 copy-done.7
  22.2 0.0 copy-done.8
  22.2 0.0 copy-done.9
  22.2 30.3 %fusion.168 = (f32[512]{0:T(512)S(1)}, f32[512,1024]{1,0:T(8,128)S(1)}) fusion(f32[1024]{0:T(1024)S(1)} %copy-done.9, bf16[4096,1024]{1,0:T(8,128)(2,1)} %param.29, bf16[512,1024]{1,0:T(8,128)(2,1)S(1)} %bitcast.84, bf16[1024,4096]{1,0:T(8,128)(2,1)} %param.27, f32[4096]{0:T(1024)S(1)} %copy-done.8), kind=kOutput, calls=%fused_computation.263 | convolution fusion | flops 8730443776 | bytes 19945472 | tf_op jit(solution)/shard_map/dot_general | solution.py:12
  52.4 0.3 multiply_reduce_fusion.1
  52.8 0.9 multiply_reduce_fusion
  53.7 0.0 copy-start.6
  53.7 0.0 copy-start.10
  53.7 1.5 multiply_convert_fusion
  55.2 0.0 copy-start.1
  55.2 0.0 copy-start.4
  55.2 0.0 copy-start.5
  55.2 0.0 all-gather.4.cloned.1.call-update
  56.5 0.0 copy-done.6
  56.6 0.0 copy-done
  56.6 1.1 gather_fusion
  57.8 12.1 %all_gather.12 = bf16[1,8,128]{2,0,1:T(2,128)(2,1)S(1)} all-gather(bf16[1,1,128]{2,0,1:T(2,128)(2,1)S(1)} %fusion.100), channel_id=1, replica_groups=mesh['dp'=8,'prompt'=16] {'dp'}, dimensions={1}, use_global_device_ids=true | all-gather | bytes 2304 | tf_op jit(solution)/shard_map/all_gather | solution.py:66
  69.8 0.0 copy-done.10
  69.8 1.6 sort.34
  71.5 0.7 gather_fusion.7
  72.2 0.7 gather_fusion.8
  72.9 0.0 copy-done.1
  72.9 0.7 gather_fusion.6
  73.6 0.0 copy-done.4
  73.6 3.1 %gather_fusion.2 = bf16[512]{0:T(512)(128)(2,1)S(1)} fusion(f32[50265]{0:T(1024)S(1)} %copy-done, s32[1024]{0:T(1024)S(1)} %pad_clamp_fusion.2), kind=kCustom, calls=%fused_computation.7 | custom fusion | bytes 4096 | tf_op jit(solution)/shard_map/jit(_take)/gather | solution.py:25
  76.7 0.0 copy-done.5
  76.8 0.1 fusion.98
  76.8 20.3 %all_gather.13 = bf16[4,16,128]{2,0,1:T(4,128)(2,1)S(1)} all-gather(bf16[4,1,128]{2,0,1:T(4,128)(2,1)S(1)} %fusion.98), channel_id=1, replica_groups=mesh['dp'=8,'prompt'=16] {'prompt'}, dimensions={1}, use_global_device_ids=true | all-gather | bytes 17408 | tf_op jit(solution)/shard_map/all_gather | solution.py:89
  97.2 1.6 sort.35
  98.8 0.6 convert_reduce_fusion.2
  99.4 0.6 gather_fusion.1
  100.0 0.6 gather_fusion.3
  100.6 0.1 broadcast_compare_fusion
  100.7 0.1 broadcast_compare_fusion.1
  100.8 0.0 all-gather.6.cloned.1.call-done
  100.8 6.9 %gather_fusion.4 = bf16[32,128,1024]{2,1,0:T(8,128)(2,1)} fusion(bf16[8,128,1024]{2,1,0:T(8,128)(2,1)} %bitcast.74, s32[1024]{0:T(1024)S(1)} %get-tuple-element.41), kind=kCustom, calls=%fused_computation.9 | custom fusion | bytes 16777344 | tf_op jit(solution)/shard_map/jit(_take)/gather | solution.py:80
  107.7 62.4 %all-gather.4.cloned.1.call-done = bf16[4,16,128,1024]{3,2,1,0:T(8,128)(2,1)} async-done(((bf16[4,1,128,1024]{3,2,1,0:T(8,128)(2,1)}), bf16[4,16,128,1024]{3,2,1,0:T(8,128)(2,1)}) %all-gather.4.cloned.1.call-update) | async-done | bytes 16777232 | tf_op jit(solution)/shard_map/all_gather | solution.py:88
  170.1 10.8 %gather_fusion.5 = bf16[32,128,1024]{2,1,0:T(8,128)(2,1)} fusion(bf16[64,128,1024]{2,1,0:T(8,128)(2,1)} %bitcast.75, s32[1024]{0:T(1024)S(1)} %get-tuple-element.40), kind=kCustom, calls=%fused_computation.10 | custom fusion | bytes 16777344 | tf_op jit(solution)/shard_map/jit(_take)/gather | solution.py:94
  180.8 7.6 %select_reduce_fusion = (f32[32,128]{1,0:T(8,128)S(1)}, f32[32,128]{1,0:T(8,128)S(1)}) fusion(pred[32,128]{1,0:T(8,128)(4,1)S(1)} %broadcast_compare_fusion, pred[32,128]{1,0:T(8,128)(4,1)S(1)} %broadcast_compare_fusion.1, bf16[32,128,1024]{2,1,0:T(8,128)(2,1)} %gather_fusion.5, pred[32]{0:T(512)(128)(4,1)S(1)} %get-tuple-element.24, ...), kind=kOutput, calls=%fused_computation.73 | convolution fusion | flops 1084219392 | bytes 16818240 | tf_op jit(solution)/shard_map/uqg,uog->uqo/dot_general | solution.py:96
  188.4 0.2 convert_reduce_fusion.1
  188.6 0.7 gather_fusion.9
  189.3 0.7 gather_fusion.10
  190.1 0.1 fusion.96
  190.2 32.2 %all-reduce = (f32[3]{0:T(128)S(1)}, f32[]{:T(128)}) all-reduce(f32[3]{0:T(128)S(1)} %fusion.96, f32[]{:T(128)} %convert_reduce_fusion.2), channel_id=1, replica_groups=mesh['dp'=8,'prompt'=16] {'prompt'}, use_global_device_ids=true, to_apply=%region_15.18 | all-reduce | flops 4 | bytes 32 | tf_op jit(solution)/shard_map/psum | solution.py:120
  222.4 20.0 %all-reduce.1 = (f32[3]{0:T(128)S(1)}, f32[]{:T(128)}) all-reduce(f32[3]{0:T(128)S(1)} %get-tuple-element.16, f32[]{:T(128)} %get-tuple-element.17), channel_id=1, replica_groups=mesh['dp'=8,'prompt'=16] {'dp'}, use_global_device_ids=true, to_apply=%region_16.19 | all-reduce | flops 4 | bytes 32 | tf_op jit(solution)/shard_map/psum | solution.py:120
  242.4 1.2 broadcast_divide_fusion
  243.5 0.6 broadcast_select_fusion.3
  (28 shorter events, 0.2 us)
Async XLA Ops:
  7.2 49.4 %copy-start = (f32[50265]{0:T(1024)S(1)}, f32[50265]{0:T(1024)}, u32[]{:S(2)}) copy-start(f32[50265]{0:T(1024)} %param.26) | copy-start | bytes 603184
  7.2 13.5 %copy-start.2 = (f32[1024]{0:T(1024)S(1)}, f32[1024]{0:T(1024)}, u32[]{:S(2)}) copy-start(f32[1024]{0:T(1024)} %param.32) | copy-start | bytes 12292
  7.2 13.5 %copy-start.3 = (f32[1024]{0:T(1024)S(1)}, f32[1024]{0:T(1024)}, u32[]{:S(2)}) copy-start(f32[1024]{0:T(1024)} %param.31) | copy-start | bytes 12292
  7.2 93.6 %all-gather.6.cloned.1.call-start = ((), (), s32[]{:S(2)}) async-start(), calls=%async_computation.1 | async-start | bytes 2359296 | tf_op jit(solution)/shard_map/all_gather | solution.py:65
  20.5 1.7 copy-start.7
  20.5 1.7 copy-start.8
  20.5 1.7 copy-start.9
  21.9 148.1 %all-gather.4.cloned.1.call-start = ((), (), s32[]{:S(2)}) async-start(), calls=%async_computation | async-start | bytes 17825792 | tf_op jit(solution)/shard_map/all_gather | solution.py:88
  53.7 2.8 %copy-start.6 = (s32[1,1,128]{2,1,0:T(1,128)S(1)}, s32[1,1,128]{2,1,0:T(1,128)}, u32[]{:S(2)}) copy-start(s32[1,1,128]{2,1,0:T(1,128)} %param.22) | copy-start | bytes 1540
  53.7 16.1 %copy-start.10 = (s32[1,1,32]{2,1,0:T(1,128)S(1)}, s32[1,1,32]{2,1,0:T(1,128)}, u32[]{:S(2)}) copy-start(s32[1,1,32]{2,1,0:T(1,128)} %param.34) | copy-start | bytes 388
  55.2 17.7 %copy-start.1 = (s32[1,1,32]{2,1,0:T(1,128)S(1)}, s32[1,1,32]{2,1,0:T(1,128)}, u32[]{:S(2)}) copy-start(s32[1,1,32]{2,1,0:T(1,128)} %param.33) | copy-start | bytes 388
  55.2 18.4 %copy-start.4 = (s32[4,1,128]{2,1,0:T(1,128)S(1)}, s32[4,1,128]{2,1,0:T(1,128)}, u32[]{:S(2)}) copy-start(s32[4,1,128]{2,1,0:T(1,128)} %param.23) | copy-start | bytes 6148
  55.2 21.6 %copy-start.5 = (s32[4,1]{0,1:T(1,128)S(1)}, s32[4,1]{0,1:T(1,128)}, u32[]{:S(2)}) copy-start(s32[4,1]{0,1:T(1,128)} %param.25) | copy-start | bytes 52
Sparse Core Ops, SparseCore 0:
  22.0 28.8 all-gather.5
  55.3 114.6 all-gather.3
